TPU v7x, 256 devices: a whole 4x4x8 slice. The times are simulated.
256 devices in a mesh: pix: 16 (over x_hi, z), peak: 16 (over y, x_lo, core).
Axes of the slice: x: 4 (x_hi: 2, x_lo: 2; x = x_hi * 2 + x_lo), y: 4, z: 8, core: 2. Of those that a mesh axis runs over, the one named last changes fastest.
Arguments:
- cube: bfloat16 [65536, 8, 2048], P('pix', None, 'peak'), may hold values from -6 to 6
- pix_factor: bfloat16 [65536, 64], P(('pix', 'peak')), may hold values from -0.8984375 to 0.8984375
- sec_factor: bfloat16 [8, 64], replicated, may hold values from -5 to 5
- peak_factor: bfloat16 [2048, 64], P('peak'), may hold values from -0.046875 to 0.046875
Outputs:
- grad_pix: float32 [65536, 64], P(('pix', 'peak'))
- grad_peak: float32 [2048, 64], P('peak')
All inputs are finite; a program needn't handle non-finite values.
Results may differ from a plain program's by a relative error of at most 0.0003.
Values may be sent and summed in bfloat16 or wider, within the bound.
No kernel may reach another device: no remote copies, remote signals or barrier semaphores. Data moves between devices by JAX's collectives and lax.ppermute only.
A program may use at most 64 MiB of HBM per device.

v0:
```python
import math
import jax
import jax.numpy as jnp
from jax import lax
from jax.sharding import PartitionSpec as P


def on_device(cube, pix_factor, sec_factor, peak_factor):
    pixels = cube.shape[0]
    sections = cube.shape[1]
    peaks = cube.shape[2]
    rank = peak_factor.shape[1]
    fb = sec_factor.astype(jnp.float32)
    fa_own = pix_factor.astype(jnp.float32)
    fc_own = peak_factor.astype(jnp.float32)
    gathered = lax.all_gather(pix_factor, "peak", axis=0, tiled=True)
    ttm = jnp.dot(
        cube.reshape(pixels * sections, peaks), peak_factor, preferred_element_type=jnp.float32
    )
    ttm = ttm.reshape(pixels, sections, rank)
    summed_pix = lax.psum_scatter(
        jnp.sum(ttm * fb[None, :, :], axis=1), "peak", scatter_dimension=0, tiled=True
    )
    partial_peak = jnp.zeros((peaks, rank), jnp.float32)
    for index in range(sections):
        inner = lax.dot_general(
            cube[:, index, :],
            gathered,
            (((0,), (0,)), ((), ())),
            preferred_element_type=jnp.float32,
        )
        partial_peak = partial_peak + inner * fb[index][None, :]
    local_a = jnp.dot(pix_factor.T, pix_factor, preferred_element_type=jnp.float32)
    local_c = jnp.dot(peak_factor.T, peak_factor, preferred_element_type=jnp.float32)
    gram_b = jnp.dot(sec_factor.T, sec_factor, preferred_element_type=jnp.float32)
    gram_a = lax.psum(local_a, ("pix", "peak"))
    gram_c = lax.psum(local_c, "peak")
    grad_pix = summed_pix - jnp.dot(fa_own, gram_b * gram_c, precision=lax.Precision.HIGHEST)
    scale = 1.0 / math.sqrt(float(sections * pixels * lax.axis_size("pix")))
    weight_c = gram_a * gram_b
    total = lax.psum(partial_peak, "pix")
    grad_peak = (total - jnp.dot(fc_own, weight_c, precision=lax.Precision.HIGHEST)) * scale
    return (grad_pix, grad_peak)


def solution(mesh):
    in_specs = (P("pix", None, "peak"), P(("pix", "peak"), None), P(), P("peak", None))
    out_specs = (P(("pix", "peak"), None), P("peak", None))
    return jax.shard_map(
        on_device, mesh=mesh, in_specs=in_specs, out_specs=out_specs, check_vma=False
    )
```

profile of v0, /device:TPU:4, one launch (start us, length us, event | category | flops | bytes accessed | tf_op | source)
XLA Modules:
  0.0 273.6 jit_solution(18076057092134265733)
XLA Ops:
  7.2 0.0 copy-start
  7.2 0.0 reduce-scatter.2.cloned.1.call-start
  7.2 0.7 convert_element_type.2
  7.9 0.0 copy-done
  7.9 7.9 %multiply_reduce_fusion = f32[4096,64]{0,1:T(8,128)} fusion(f32[8,64]{1,0:T(8,128)S(1)} %convert_element_type.2, bf16[128,64]{0,1:T(8,128)(2,1)S(1)} %copy-done, bf16[4096,8,128]{2,1,0:T(8,128)(2,1)} %param.4), kind=kOutput, calls=%fused_computation | convolution fusion | flops 540803072 | bytes 9455616 | tf_op jit(solution)/shard_map/dot_general | solution.py:17
  15.9 0.0 reduce-scatter.2.cloned.1.call-update
  15.9 0.0 copy-start.1
  15.9 7.7 %copy.7 = bf16[4096,8,128]{2,0,1:T(8,128)(2,1)} copy(bf16[4096,8,128]{2,1,0:T(8,128)(2,1)} %param.4) | data formatting | bytes 16777216 | tf_op args[0]
  23.6 0.0 copy-done.1
  23.6 0.0 copy-start.2
  23.6 23.0 %all_gather.3 = bf16[4096,64]{0,1:T(8,128)(2,1)S(1)} all-gather(bf16[256,64]{0,1:T(8,128)(2,1)S(1)} %copy-done.1), channel_id=1, replica_groups=mesh['pix'=16,'peak'=16] {'peak'}, dimensions={0}, use_global_device_ids=true | all-gather | bytes 557056 | tf_op jit(solution)/shard_map/all_gather | solution.py:16
  46.6 0.1 fusion.16
  46.7 0.1 fusion.15
  46.8 1.6 convolution_multiply_fusion.7
  48.4 1.5 fusion.7
  50.0 77.0 %psum.23 = f32[64,64]{1,0:T(8,128)S(1)} all-reduce(f32[64,64]{1,0:T(8,128)S(1)} %fusion.16), channel_id=1, replica_groups=mesh['pix'=16,'peak'=16] {'pix','peak'}, use_global_device_ids=true, to_apply=%region_4.0 | all-reduce | flops 4096 | bytes 32768 | tf_op jit(solution)/shard_map/psum | solution.py:36
  126.9 53.7 %psum.21 = f32[64,64]{1,0:T(8,128)S(1)} all-reduce(f32[64,64]{1,0:T(8,128)S(1)} %fusion.15), channel_id=1, replica_groups=mesh['pix'=16,'peak'=16] {'peak'}, use_global_device_ids=true, to_apply=%region_2.0 | all-reduce | flops 4096 | bytes 32768 | tf_op jit(solution)/shard_map/psum | solution.py:37
  180.6 1.5 fusion.6
  182.2 1.5 fusion.5
  183.7 1.5 fusion.4
  185.3 1.5 fusion.3
  186.8 1.5 fusion.2
  188.3 1.5 fusion.1
  189.9 74.1 %psum.22 = f32[128,64]{0,1:T(8,128)S(1)} all-reduce(f32[128,64]{0,1:T(8,128)S(1)} %fusion.1), channel_id=1, replica_groups=mesh['pix'=16,'peak'=16] {'pix'}, use_global_device_ids=true, to_apply=%region_3.0 | all-reduce | flops 8192 | bytes 65536 | tf_op jit(solution)/shard_map/psum | solution.py:41
  264.0 0.0 copy-done.2
  264.0 0.2 fusion.14
  264.2 0.8 fusion.9
  265.1 0.0 reduce-scatter.2.cloned.1.call-done
  265.1 1.7 fusion
  (1 shorter events, 0.0 us)
Async XLA Ops:
  7.2 0.8 copy-start
  7.2 257.9 %reduce-scatter.2.cloned.1.call-start = ((), (), s32[]{:S(2)}) async-start(), calls=%async_computation.1 | async-start | bytes 1114112 | tf_op jit(solution)/shard_map/reduce_scatter | solution.py:21
  15.9 7.7 %copy-start.1 = (bf16[256,64]{0,1:T(8,128)(2,1)S(1)}, bf16[256,64]{0,1:T(8,128)(2,1)}, u32[]{:S(2)}) copy-start(bf16[256,64]{0,1:T(8,128)(2,1)} %param.5) | copy-start | bytes 98308
  23.6 240.4 %copy-start.2 = (bf16[8,64]{1,0:T(8,128)(2,1)S(1)}, bf16[8,64]{1,0:T(8,128)(2,1)}, u32[]{:S(2)}) copy-start(bf16[8,64]{1,0:T(8,128)(2,1)} %param.6) | copy-start | bytes 3076
Sparse Core Ops, SparseCore 0:
  16.0 66.9 reduce-scatter.1
where the time goes:
time: 274 us
  blocking collectives  228 us (83%)
  matrix products  23.3 us (9%)
  between operations  14.1 us (5%)
  local copies, waits for them, and re-layouts  7.72 us (3%)
    psum x1, blocking collectives, on_device(): gram_a = lax.psum(local_a, ('pix', 'peak'))  77 us
    psum x1, blocking collectives, on_device(): total = lax.psum(partial_peak, 'pix')  74.1 us
    psum x1, blocking collectives, on_device(): gram_c = lax.psum(local_c, 'peak')  53.7 us
    all_gather x1, blocking collectives, on_device(): gathered = lax.all_gather(pix_factor, 'peak', axis=0, tiled=True)  23 us
    dot_general x8, matrix products, on_device(): lax.dot_general(cube[:, index, :], gathered, (((0,), (0,)), ((), ())), pr...  12.4 us
    dot_general x1, matrix products, on_device(): jnp.dot(cube.reshape(pixels * sections, peaks), peak_factor, preferred_el...  7.95 us
    unnamed x7, local copies, waits for them, and re-layouts  7.71 us
  transfers between devices with their start and end apart: 1, of which 0 were waited for; matrix products, arithmetic and copies ran while one was open for 8% of the time, Pallas kernels for 0%

commit v1 on v0

--- a/solution.py
+++ b/solution.py
@@ -33,7 +33,7 @@
     local_a = jnp.dot(pix_factor.T, pix_factor, preferred_element_type=jnp.float32)
     local_c = jnp.dot(peak_factor.T, peak_factor, preferred_element_type=jnp.float32)
     gram_b = jnp.dot(sec_factor.T, sec_factor, preferred_element_type=jnp.float32)
-    gram_a = lax.psum(local_a, ("pix", "peak"))
+    gram_a = lax.psum(lax.psum(local_a, "pix"), "peak")
     gram_c = lax.psum(local_c, "peak")
     grad_pix = summed_pix - jnp.dot(fa_own, gram_b * gram_c, precision=lax.Precision.HIGHEST)
     scale = 1.0 / math.sqrt(float(sections * pixels * lax.axis_size("pix")))

time: 274 us -> 200 us (0.73)
  blocking collectives: 228 us -> 153 us
    psum x2 -> x1, blocking collectives: 151 us -> 77 us  [on_device(): gram_a = lax.psum(lax.psum(local_a, 'pix'), 'peak')]
  transfers between devices with their start and end apart: 1 -> 1, of which waited for: 0 -> 0; matrix products, arithmetic and copies ran while one was open for 8% -> 11% of each run, Pallas kernels for 0% -> 0%
where the time goes in v1:
time: 200 us; the launch traced here: 199 us
  blocking collectives  153 us (76%)
  matrix products  23.4 us (12%)
  between operations  14.1 us (7%)
  local copies, waits for them, and re-layouts  7.72 us (4%)
    psum x1, blocking collectives, on_device(): gram_a = lax.psum(lax.psum(local_a, 'pix'), 'peak')  77 us
    psum x1, blocking collectives, on_device(): gram_c = lax.psum(local_c, 'peak')  53 us
    all_gather x1, blocking collectives, on_device(): gathered = lax.all_gather(pix_factor, 'peak', axis=0, tiled=True)  23 us
    dot_general x8, matrix products, on_device(): lax.dot_general(cube[:, index, :], gathered, (((0,), (0,)), ((), ())), pr...  12.5 us
    dot_general x1, matrix products, on_device(): jnp.dot(cube.reshape(pixels * sections, peaks), peak_factor, preferred_el...  7.95 us
    unnamed x7, local copies, waits for them, and re-layouts  7.71 us
  transfers between devices with their start and end apart: 1, of which 0 were waited for; matrix products, arithmetic and copies ran while one was open for 11% of the time, Pallas kernels for 0%

profile of v1, /device:TPU:4, one launch (start us, length us, event | category | flops | bytes accessed | tf_op | source)
XLA Modules:
  0.0 198.9 jit_solution(15722556940227349827)
XLA Ops:
  7.2 0.0 copy-start
  7.2 0.0 reduce-scatter.2.cloned.1.call-start
  7.2 0.7 convert_element_type.2
  7.9 0.0 copy-done
  7.9 7.9 %multiply_reduce_fusion = f32[4096,64]{0,1:T(8,128)} fusion(f32[8,64]{1,0:T(8,128)S(1)} %convert_element_type.2, bf16[128,64]{0,1:T(8,128)(2,1)S(1)} %copy-done, bf16[4096,8,128]{2,1,0:T(8,128)(2,1)} %param.4), kind=kOutput, calls=%fused_computation | convolution fusion | flops 540803072 | bytes 9455616 | tf_op jit(solution)/shard_map/dot_general | solution.py:17
  15.9 0.0 reduce-scatter.2.cloned.1.call-update
  15.9 0.0 copy-start.1
  15.9 7.7 %copy.7 = bf16[4096,8,128]{2,0,1:T(8,128)(2,1)} copy(bf16[4096,8,128]{2,1,0:T(8,128)(2,1)} %param.4) | data formatting | bytes 16777216 | tf_op args[0]
  23.6 0.0 copy-done.1
  23.6 0.0 copy-start.2
  23.6 23.0 %all_gather.3 = bf16[4096,64]{0,1:T(8,128)(2,1)S(1)} all-gather(bf16[256,64]{0,1:T(8,128)(2,1)S(1)} %copy-done.1), channel_id=1, replica_groups=mesh['pix'=16,'peak'=16] {'peak'}, dimensions={0}, use_global_device_ids=true | all-gather | bytes 557056 | tf_op jit(solution)/shard_map/all_gather | solution.py:16
  46.6 1.5 convolution_multiply_fusion.7
  48.1 1.6 fusion.7
  49.7 1.6 fusion.6
  51.3 0.1 fusion.16
  51.4 1.6 fusion.5
  53.0 1.6 fusion.4
  54.5 1.6 fusion.3
  56.1 1.6 fusion.2
  57.7 1.6 fusion.1
  59.2 77.0 %all-reduce.1 = (f32[64,64]{1,0:T(8,128)S(1)}, f32[128,64]{0,1:T(8,128)S(1)}) all-reduce(f32[64,64]{1,0:T(8,128)S(1)} %fusion.16, f32[128,64]{0,1:T(8,128)S(1)} %fusion.1), channel_id=1, replica_groups=mesh['pix'=16,'peak'=16] {'pix'}, use_global_device_ids=true, to_apply=%region_4.0 | all-reduce | flops 12288 | bytes 98304 | tf_op jit(solution)/shard_map/psum | solution.py:36
  136.2 0.1 fusion.15
  136.3 53.0 %all-reduce = (f32[64,64]{1,0:T(8,128)S(1)}, f32[64,64]{1,0:T(8,128)S(1)}) all-reduce(f32[64,64]{1,0:T(8,128)S(1)} %fusion.15, f32[64,64]{1,0:T(8,128)S(1)} %get-tuple-element.4), channel_id=1, replica_groups=mesh['pix'=16,'peak'=16] {'peak'}, use_global_device_ids=true, to_apply=%region_2.0 | all-reduce | flops 8192 | bytes 65536 | tf_op jit(solution)/shard_map/psum | solution.py:37
  189.3 0.0 copy-done.2
  189.3 0.2 fusion.14
  189.5 0.8 fusion.9
  190.3 0.0 reduce-scatter.2.cloned.1.call-done
  190.3 1.7 fusion
  (1 shorter events, 0.0 us)
Async XLA Ops:
  7.2 0.8 copy-start
  7.2 183.1 %reduce-scatter.2.cloned.1.call-start = ((), (), s32[]{:S(2)}) async-start(), calls=%async_computation.1 | async-start | bytes 1114112 | tf_op jit(solution)/shard_map/reduce_scatter | solution.py:21
  15.9 7.7 %copy-start.1 = (bf16[256,64]{0,1:T(8,128)(2,1)S(1)}, bf16[256,64]{0,1:T(8,128)(2,1)}, u32[]{:S(2)}) copy-start(bf16[256,64]{0,1:T(8,128)(2,1)} %param.5) | copy-start | bytes 98308
  23.6 165.7 %copy-start.2 = (bf16[8,64]{1,0:T(8,128)(2,1)S(1)}, bf16[8,64]{1,0:T(8,128)(2,1)}, u32[]{:S(2)}) copy-start(bf16[8,64]{1,0:T(8,128)(2,1)} %param.6) | copy-start | bytes 3076
Sparse Core Ops, SparseCore 0:
  16.0 67.1 reduce-scatter.1
